TPU v7x, 512 devices: a whole 4x8x8 slice. The times are simulated.
512 devices in a mesh: tm: 32 (over x, z), space: 16 (over y, core).
Axes of the slice: x: 4, y: 8, z: 8, core: 2. Of those that a mesh axis runs over, the one named last changes fastest.
Arguments:
- inverse_factor: bfloat16 [32, 2048, 2048], P('tm', None, 'space'), as said below
- arrow_factor: bfloat16 [32, 64, 2048], P('tm', None, 'space'), may hold values from -6 to 6
- decay: float32 [32, 2048], P('tm'), may hold values from 0 to 1
- tip_inverse: float32 [64, 64], replicated, may hold values from -0.75 to 0.75
- sigma_end: float32 [2048, 2048], P(None, 'space'), may hold values from -2.7 to 2.7, as said below
- arrow_end: float32 [2048, 64], P('space'), may hold values from -6 to 6
Outputs:
- sigmas: float32 [32, 2048, 2048], P('tm', None, 'space')
- arrows: float32 [32, 2048, 64], P('tm', 'space')
Inputs may be any that keep to these rules, and one draw needn't show every extreme that they name: `inverse_factor`: each K_t is lower triangular with a positive diagonal. `sigma_end`: symmetric.
All inputs are finite; a program needn't handle non-finite values.
Results may differ from a plain program's by a relative error of at most 0.0003.
Values may be sent and summed in bfloat16 or wider, within the bound.
No kernel may reach another device: no remote copies, remote signals or barrier semaphores. Data moves between devices by JAX's collectives and lax.ppermute only.
A program may use at most 128 MiB of HBM per device.

v0:
```python
import jax
import jax.numpy as jnp
from jax import lax
from jax.sharding import PartitionSpec as P


def prefix(array, axis, combine, identity):
    devices, position = (lax.axis_size(axis), lax.axis_index(axis))
    everything = jax.tree.map(lambda part: lax.all_gather(part, axis), array)
    start = jax.tree.map(
        lambda part, zero: jnp.broadcast_to(jnp.asarray(zero, part.dtype), part.shape),
        array,
        identity,
    )

    def hop(k, before):
        at = devices - 1 - k
        reached = at > position
        new = combine(before, jax.tree.map(lambda part: part[at], everything))
        return jax.tree.map(lambda a, b: jnp.where(reached, a, b), new, before)

    return lax.fori_loop(0, devices, hop, start)


def column_products(left, right):
    return lax.dot_general(
        left, right, (((0,), (0,)), ((), ())), preferred_element_type=jnp.float32
    )


def compose(earlier, later):
    falloff_later, own_after, sigma_after, arrow_after = earlier
    lower_factor_current, own_here, sigma_here, border_column_current = later
    return (
        lower_factor_current * falloff_later,
        own_here * own_after,
        sigma_here + lower_factor_current[:, None] * own_here[None, :] * sigma_after,
        border_column_current + own_here[:, None] * arrow_after,
    )


def body(inverse_factor, arrow_factor, decay, tip_inverse, sigma_end, arrow_end):
    highest = lax.Precision.HIGHEST
    factor_cols = inverse_factor[0]
    order = factor_cols.shape[0]
    width = factor_cols.shape[1]
    panel_index = lax.axis_index("space")
    precision_panel = column_products(
        lax.all_gather(factor_cols, "space", axis=1, tiled=True), factor_cols
    )
    decay_all = decay[0]
    self_falloff = lax.dynamic_slice_in_dim(decay_all, panel_index * width, width)
    arrow_local = arrow_factor[0]
    arrow_wide = arrow_local.astype(jnp.float32)
    cross = lax.psum_scatter(
        lax.dot_general(
            precision_panel,
            arrow_wide,
            (((1,), (1,)), ((), ())),
            precision=highest,
            preferred_element_type=jnp.float32,
        ),
        "space",
        scatter_dimension=0,
        tiled=True,
    )
    own_arrow = -jnp.dot(cross, tip_inverse, precision=highest)
    arrow_cols_count = tip_inverse.shape[0]
    identity_matrix = (
        jnp.ones((order,), jnp.float32),
        jnp.ones((width,), jnp.float32),
        jnp.zeros((order, width), jnp.float32),
        jnp.zeros((width, arrow_cols_count), jnp.float32),
    )
    mine = (decay_all, self_falloff, precision_panel, own_arrow)
    later_decay, later_own, later_sigma, later_arrow = prefix(mine, "tm", compose, identity_matrix)
    covariance_following = later_sigma + later_decay[:, None] * later_own[None, :] * sigma_end
    spike_ahead = later_arrow + later_own[:, None] * arrow_end
    sigma_block = (
        precision_panel + decay_all[:, None] * self_falloff[None, :] * covariance_following
    )
    arrow_block = own_arrow + self_falloff[:, None] * spike_ahead
    return (sigma_block[None], arrow_block[None])


def solution(mesh):
    placed = (
        P("tm", None, "space"),
        P("tm", None, "space"),
        P("tm", None),
        P(),
        P(None, "space"),
        P("space", None),
    )
    return jax.shard_map(
        body,
        mesh=mesh,
        in_specs=placed,
        out_specs=(P("tm", None, "space"), P("tm", "space", None)),
        check_vma=False,
    )
```

profile of v0, /device:TPU:1, one launch (start us, length us, event | category | flops | bytes accessed | tf_op | source)
XLA Modules:
  0.0 611.4 jit_solution(3542080441122480926)
XLA Ops:
  8.0 76.7 %all-gather.9.cloned.1.call-done = bf16[1,2048,2048]{2,1,0:T(8,128)(2,1)} async-done(((bf16[1,2048,128]{2,1,0:T(8,128)(2,1)}), bf16[1,2048,2048]{2,1,0:T(8,128)(2,1)}) %all-gather.9.cloned.1.call-update) | async-done | bytes 8388624 | tf_op jit(solution)/shard_map/all_gather | solution.py:49
  84.7 5.8 fusion.3
  92.2 54.2 %reduce-scatter.2.cloned.1.call-done = f32[128,64]{1,0:T(8,128)} async-done(((f32[2048,64]{1,0:T(8,128)}), f32[128,64]{1,0:T(8,128)}) %reduce-scatter.2.cloned.1.call-update) | async-done | bytes 32784 | tf_op jit(solution)/shard_map/reduce_scatter | solution.py:55
  148.8 37.9 %all-gather.3 = f32[32,1,2048]{2,1,0:T(1,128)S(1)} all-gather(f32[1,1,2048]{2,1,0:T(1,128)S(1)} %bitcast.51), channel_id=1, replica_groups=mesh['tm'=32,'space'=16] {'tm'}, dimensions={0}, use_global_device_ids=true | all-gather | bytes 270336 | tf_op jit(solution)/shard_map/all_gather | solution.py:9
  187.4 33.0 %all-gather.4 = f32[32,1,128]{2,1,0:T(1,128)} all-gather(f32[1,1,128]{2,1,0:T(1,128)S(1)} %get-tuple-element.327), channel_id=1, replica_groups=mesh['tm'=32,'space'=16] {'tm'}, dimensions={0}, use_global_device_ids=true | all-gather | bytes 16896 | tf_op jit(solution)/shard_map/all_gather | solution.py:9
  220.4 4.0 all-gather.13.cloned.1.call-done
  224.4 3.1 copy.12
  227.5 243.0 %all-gather.11.cloned.1.call-done = f32[65536,128]{1,0:T(8,128)} async-done(((f32[2048,128]{1,0:T(8,128)}), f32[65536,128]{1,0:T(8,128)}) %all-gather.11.cloned.1.call-update) | async-done | bytes 33554448 | tf_op jit(solution)/shard_map/all_gather | solution.py:9
  470.5 130.7 %while.22 = (s32[]{:T(128)}, f32[2048]{0:T(1024)S(1)}, f32[128]{0:T(128)}, f32[2048,128]{1,0:T(8,128)S(1)}, f32[128,64]{1,0:T(8,128)S(1)}, /*index=5*/s32[]{:T(1...) while((s32[]{:T(128)}, f32[2048]{0:T(1024)S(1)}, ...), condition=%wide.region_2.3_spmd.clone, body=%wide.region_1.2_spmd.clone.sunk | while | flops 1350024 | bytes 3296485 | solution.py:22
  472.9 1.8 fusion.16
  477.0 1.8 fusion.16
  481.1 1.8 fusion.16
  485.2 1.8 fusion.16
  489.3 1.8 fusion.16
  493.3 1.8 fusion.16
  497.4 1.8 fusion.16
  501.5 1.8 fusion.16
  505.6 1.8 fusion.16
  509.7 1.8 fusion.16
  513.8 1.8 fusion.16
  517.8 1.8 fusion.16
  521.9 1.8 fusion.16
  526.0 1.8 fusion.16
  602.7 2.2 add_bitcast_fusion
  (178 shorter events, 111.0 us)
Async XLA Ops:
  7.2 139.2 %copy-start = (f32[64,64]{1,0:T(8,128)S(1)}, f32[64,64]{1,0:T(8,128)}, u32[]{:S(2)}) copy-start(f32[64,64]{1,0:T(8,128)} %param.11) | copy-start | bytes 49156
  7.2 83.3 %copy-start.6 = (bf16[1,64,128]{2,1,0:T(8,128)(2,1)S(1)}, bf16[1,64,128]{2,1,0:T(8,128)(2,1)}, u32[]{:S(2)}) copy-start(bf16[1,64,128]{2,1,0:T(8,128)(2,1)} %param.9) | copy-start | bytes 49156
  7.2 77.5 %all-gather.9.cloned.1.call-start = ((), (), s32[]{:S(2)}) async-start(), calls=%async_computation.2 | async-start | bytes 8912896 | tf_op jit(solution)/shard_map/all_gather | solution.py:49
  7.9 140.9 %copy-start.5 = (f32[1,2048]{1,0:T(1,128)S(1)}, f32[1,2048]{1,0:T(1,128)}, u32[]{:S(2)}) copy-start(f32[1,2048]{1,0:T(1,128)} %param.10) | copy-start | bytes 24580
  7.9 138.5 %reduce-scatter.2.cloned.1.call-start = ((), (), s32[]{:S(2)}) async-start(), calls=%async_computation.1 | async-start | bytes 1114112 | tf_op jit(solution)/shard_map/reduce_scatter | solution.py:55
  90.5 57.7 %copy-start.1 = (f32[2048,128]{1,0:T(8,128)}, f32[2048,128]{1,0:T(8,128)S(1)}, u32[]{:S(2)}) copy-start(f32[2048,128]{1,0:T(8,128)S(1)} %fusion.3) | copy-start | bytes 3145732
  92.1 132.3 %all-gather.13.cloned.1.call-start = ((), (), s32[]{:S(2)}) async-start(), calls=%async_computation.4 | async-start | bytes 1081344 | tf_op jit(solution)/shard_map/all_gather | solution.py:9
  148.1 322.3 %all-gather.11.cloned.1.call-start = ((), (), s32[]{:S(2)}) async-start(), calls=%async_computation.3 | async-start | bytes 34603008 | tf_op jit(solution)/shard_map/all_gather | solution.py:9
  470.5 130.8 %copy-start.4 = (f32[128,64]{0,1:T(8,128)S(1)}, f32[128,64]{0,1:T(8,128)}, u32[]{:S(2)}) copy-start(f32[128,64]{0,1:T(8,128)} %convolution_negate_fusion) | copy-start | bytes 98308
  470.5 132.2 %copy-start.2 = (f32[2048,128]{1,0:T(8,128)S(1)}, f32[2048,128]{1,0:T(8,128)}, u32[]{:S(2)}) copy-start(f32[2048,128]{1,0:T(8,128)} %copy-done.1) | copy-start | bytes 3145732
  470.5 132.2 %copy-start.3 = (f32[2048,128]{1,0:T(8,128)S(1)}, f32[2048,128]{1,0:T(8,128)}, u32[]{:S(2)}) copy-start(f32[2048,128]{1,0:T(8,128)} %param.12) | copy-start | bytes 3145732
Sparse Core Ops, SparseCore 0:
  10.1 74.5 all-gather.8
  92.2 54.1 reduce-scatter.1
  150.5 73.8 all-gather.12
  228.5 241.9 all-gather.10
where the time goes:
time: 615 us; the launch traced here: 611 us
  waiting for transfers between devices  379 us (62%)
  other arithmetic  132 us (21%)
  blocking collectives  70.9 us (12%)
  between operations  13.9 us (2%)
  matrix products  9.12 us (1%)
    all_gather x2, waiting for transfers between devices, prefix(): everything = jax.tree.map(lambda part: lax.all_gather(part, axis), array)  247 us
    select_n x128, other arithmetic, hop(): return jax.tree.map(lambda a, b: jnp.where(reached, a, b), new, before)  129 us
    all_gather x1, waiting for transfers between devices, body(): lax.all_gather(factor_cols, 'space', axis=1, tiled=True)  76.7 us
    all_gather x2, blocking collectives, prefix(): everything = jax.tree.map(lambda part: lax.all_gather(part, axis), array)  70.9 us
    reduce_scatter x1, waiting for transfers between devices, body(): lax.psum_scatter(lax.dot_general(precision_panel, arrow_wide, (((1,), (1,...  54.2 us
  transfers between devices with their start and end apart: 4, of which 4 were waited for; matrix products, arithmetic and copies ran while one was open for 1% of the time, Pallas kernels for 0%

commit v1 on v0

--- a/solution.py
+++ b/solution.py
@@ -2,6 +2,28 @@
 import jax.numpy as jnp
 from jax import lax
 from jax.sharding import PartitionSpec as P
+
+
+def in_order(blocks, dim):
+    blocks = jnp.moveaxis(blocks, 0, dim)
+    dims = blocks.shape
+    return blocks.reshape(*dims[:dim], dims[dim] * dims[dim + 1], *dims[dim + 2 :])
+
+
+def collect(x, axis, dim):
+    length = lax.axis_size(axis)
+    pairs = [(i, (i + 1) % length) for i in range(length)]
+    back = [(b, a) for a, b in pairs]
+    lower, upper = ([], [])
+    for lap in range(length - 1):
+        if lap % 2 == 0:
+            lower.append(lax.ppermute(lower[-1] if lower else x, axis, pairs))
+        else:
+            upper.append(lax.ppermute(upper[-1] if upper else x, axis, back))
+    blocks = jnp.stack([*lower[::-1], x, *upper])
+    shift = lax.axis_index(axis) - len(lower)
+    blocks = blocks[(jnp.arange(length) - shift) % length]
+    return in_order(blocks, dim)
 
 
 def prefix(array, axis, combine, identity):
@@ -45,9 +67,7 @@
     order = factor_cols.shape[0]
     width = factor_cols.shape[1]
     panel_index = lax.axis_index("space")
-    precision_panel = column_products(
-        lax.all_gather(factor_cols, "space", axis=1, tiled=True), factor_cols
-    )
+    precision_panel = column_products(collect(factor_cols, "space", 1), factor_cols)
     decay_all = decay[0]
     self_falloff = lax.dynamic_slice_in_dim(decay_all, panel_index * width, width)
     arrow_local = arrow_factor[0]

time: 615 us -> 665 us (1.081)
  starting transfers between devices: 0.16 us -> 60.3 us
  waiting for transfers between devices: 379 us -> 328 us
  local copies, waits for them, and re-layouts: 4.25 us -> 47 us
    all_gather x1 -> x0, waiting for transfers between devices: 76.7 us -> none  [body(): lax.all_gather(factor_cols, 'space', axis=1, tiled=True)]
    ppermute x0 -> x15, starting transfers between devices: none -> 60.2 us  [the longest x7 52.7 us: collect(): upper.append(lax.ppermute(upper[-1] if upper else x, axis, back))]
    unnamed x16 -> x47, local copies, waits for them, and re-layouts: 3.28 us -> 24.7 us
    ppermute x0 -> x15, waiting for transfers between devices: none -> 16 us  [the longest x8 10.9 us: collect(): lower.append(lax.ppermute(lower[-1] if lower else x, axis, pairs))]
    transpose x0 -> x1, local copies, waits for them, and re-layouts: none -> 12.3 us  [in_order(): blocks = jnp.moveaxis(blocks, 0, dim)]
    reduce_scatter x1, waiting for transfers between devices: 54.2 us -> 64 us  [body(): lax.psum_scatter(lax.dot_general(precision_panel, arrow_wide, (((1,), (1,...]
    gather x0 -> x1, local copies, waits for them, and re-layouts: none -> 8.17 us  [collect(): blocks = blocks[(jnp.arange(length) - shift) % length]]
  transfers between devices with their start and end apart: 4 -> 18, of which waited for: 4 -> 14; matrix products, arithmetic and copies ran while one was open for 1% -> 4% of each run, Pallas kernels for 0% -> 0%
where the time goes in v1:
time: 665 us; the launch traced here: 660 us
  waiting for transfers between devices  328 us (49%)
  other arithmetic  130 us (20%)
  blocking collectives  70.9 us (11%)
  starting transfers between devices  60.3 us (9%)
  local copies, waits for them, and re-layouts  47 us (7%)
  between operations  13.9 us (2%)
  matrix products  8.89 us (1%)
    all_gather x2, waiting for transfers between devices, prefix(): everything = jax.tree.map(lambda part: lax.all_gather(part, axis), array)  247 us
    select_n x128, other arithmetic, hop(): return jax.tree.map(lambda a, b: jnp.where(reached, a, b), new, before)  126 us
    all_gather x2, blocking collectives, prefix(): everything = jax.tree.map(lambda part: lax.all_gather(part, axis), array)  70.9 us
    reduce_scatter x1, waiting for transfers between devices, body(): lax.psum_scatter(lax.dot_general(precision_panel, arrow_wide, (((1,), (1,...  64 us
    ppermute x7, starting transfers between devices, collect(): upper.append(lax.ppermute(upper[-1] if upper else x, axis, back))  52.7 us
    unnamed x47, local copies, waits for them, and re-layouts  24.7 us
  transfers between devices with their start and end apart: 18, of which 14 were waited for; matrix products, arithmetic and copies ran while one was open for 4% of the time, Pallas kernels for 0%

profile of v1, /device:TPU:1, one launch (start us, length us, event | category | flops | bytes accessed | tf_op | source)
XLA Modules:
  0.0 660.3 jit_solution(1558700467834395332)
XLA Ops:
  7.2 2.7 collective-permute-start
  9.9 6.4 collective-permute-done
  16.4 2.4 collective-permute-start.1
  18.8 5.4 collective-permute-start.8
  27.6 6.6 collective-permute-start.9
  36.2 7.7 %collective-permute-start.10 = (bf16[2048,128]{1,0:T(8,128)(2,1)S(1)}, bf16[2048,128]{1,0:T(8,128)(2,1)S(1)}, u32[]{:S(2)}, u32[]{:S(2)}) collective-permute-start(bf16[2048,128]{1,0:T(8,128)(2,1)S(1)} %collective-permute-done.9), channel_id=1, source_target_pairs={{1,0},{2,1},{3,2},{4,3},{5,4},{6,5},{7,6},{8,7},{9,8},{10,9},{11,1... | collective-permute-start | bytes 1572872 | tf_op jit(solution)/shard_map/ppermute | solution.py:22
  46.2 8.3 %collective-permute-start.11 = (bf16[2048,128]{1,0:T(8,128)(2,1)S(1)}, bf16[2048,128]{1,0:T(8,128)(2,1)S(1)}, u32[]{:S(2)}, u32[]{:S(2)}) collective-permute-start(bf16[2048,128]{1,0:T(8,128)(2,1)S(1)} %collective-permute-done.10), channel_id=1, source_target_pairs={{1,0},{2,1},{3,2},{4,3},{5,4},{6,5},{7,6},{8,7},{9,8},{10,9},{11,1... | collective-permute-start | bytes 1572872 | tf_op jit(solution)/shard_map/ppermute | solution.py:22
  56.8 8.2 %collective-permute-start.12 = (bf16[2048,128]{1,0:T(8,128)(2,1)S(1)}, bf16[2048,128]{1,0:T(8,128)(2,1)}, u32[]{:S(2)}, u32[]{:S(2)}) collective-permute-start(bf16[2048,128]{1,0:T(8,128)(2,1)S(1)} %collective-permute-done.11), channel_id=1, source_target_pairs={{1,0},{2,1},{3,2},{4,3},{5,4},{6,5},{7,6},{8,7},{9,8},{10,9},{11,1... | collective-permute-start | bytes 1572872 | tf_op jit(solution)/shard_map/ppermute | solution.py:22
  66.7 8.1 %collective-permute-start.13 = (bf16[2048,128]{1,0:T(8,128)(2,1)}, bf16[2048,128]{1,0:T(8,128)(2,1)}, u32[]{:S(2)}, u32[]{:S(2)}) collective-permute-start(bf16[2048,128]{1,0:T(8,128)(2,1)} %collective-permute-done.12), channel_id=1, source_target_pairs={{1,0},{2,1},{3,2},{4,3},{5,4},{6,5},{7,6},{8,7},{9,8},{10,9},{11,1... | collective-permute-start | bytes 1572872 | tf_op jit(solution)/shard_map/ppermute | solution.py:22
  76.8 8.4 %collective-permute-start.14 = (bf16[2048,128]{1,0:T(8,128)(2,1)}, bf16[2048,128]{1,0:T(8,128)(2,1)S(1)}, u32[]{:S(2)}, u32[]{:S(2)}) collective-permute-start(bf16[2048,128]{1,0:T(8,128)(2,1)} %collective-permute-done.13), channel_id=1, source_target_pairs={{1,0},{2,1},{3,2},{4,3},{5,4},{6,5},{7,6},{8,7},{9,8},{10,9},{11,1... | collective-permute-start | bytes 1572872 | tf_op jit(solution)/shard_map/ppermute | solution.py:22
  87.0 1.9 bitcast_dynamic-update-slice_fusion.13
  92.6 1.9 bitcast_dynamic-update-slice_fusion.10
  103.0 1.9 bitcast_dynamic-update-slice_fusion.1
  105.8 8.2 %gather_fusion = bf16[16,2048,128]{2,1,0:T(8,128)(2,1)} fusion(bf16[16,2048,128]{2,1,0:T(8,128)(2,1)} %bitcast_dynamic-update-slice_fusion, s32[1024]{0:T(1024)S(1)} %pad_clamp_fusion), kind=kCustom, calls=%fused_computation | custom fusion | bytes 16777280 | tf_op jit(solution)/shard_map/gather | solution.py:25
  114.0 12.3 %copy.15 = bf16[2048,16,128]{0,2,1:T(8,128)(2,1)} copy(bf16[2048,16,128]{2,0,1:T(8,128)(2,1)} %bitcast.78) | data formatting | bytes 16777216 | tf_op jit(solution)/shard_map/transpose | solution.py:8
  126.3 5.7 fusion.9
  133.7 64.0 %reduce-scatter.2.cloned.1.call-done = f32[128,64]{0,1:T(8,128)} async-done(((f32[2048,64]{0,1:T(8,128)}), f32[128,64]{0,1:T(8,128)}) %reduce-scatter.2.cloned.1.call-update) | async-done | bytes 32784 | tf_op jit(solution)/shard_map/reduce_scatter | solution.py:75
  200.2 37.8 %all-gather.2 = f32[32,1,2048]{2,1,0:T(1,128)S(1)} all-gather(f32[1,1,2048]{2,1,0:T(1,128)S(1)} %bitcast.87), channel_id=1, replica_groups=mesh['tm'=32,'space'=16] {'tm'}, dimensions={0}, use_global_device_ids=true | all-gather | bytes 270336 | tf_op jit(solution)/shard_map/all_gather | solution.py:31
  238.7 33.1 %all-gather.3 = f32[32,1,128]{2,1,0:T(1,128)} all-gather(f32[1,1,128]{2,1,0:T(1,128)S(1)} %get-tuple-element.347), channel_id=1, replica_groups=mesh['tm'=32,'space'=16] {'tm'}, dimensions={0}, use_global_device_ids=true | all-gather | bytes 16896 | tf_op jit(solution)/shard_map/all_gather | solution.py:31
  271.7 4.0 all-gather.9.cloned.1.call-done
  275.7 3.2 copy.18
  278.9 243.1 %all-gather.7.cloned.1.call-done = f32[65536,128]{1,0:T(8,128)} async-done(((f32[2048,128]{1,0:T(8,128)}), f32[65536,128]{1,0:T(8,128)}) %all-gather.7.cloned.1.call-update) | async-done | bytes 33554448 | tf_op jit(solution)/shard_map/all_gather | solution.py:31
  522.0 128.1 %while.22 = (s32[]{:T(128)}, f32[2048]{0:T(1024)S(1)}, f32[128]{0:T(128)}, f32[2048,128]{1,0:T(8,128)S(1)}, f32[128,64]{1,0:T(8,128)S(1)}, /*index=5*/s32[]{:T(1...) while((s32[]{:T(128)}, f32[2048]{0:T(1024)S(1)}, ...), condition=%wide.region_2.3_spmd.clone, body=%wide.region_1.2_spmd.clone.sunk | while | flops 1350024 | bytes 3296485 | solution.py:44
  651.6 2.2 add_bitcast_fusion
  (241 shorter events, 161.3 us)
Async XLA Ops:
  7.2 190.6 %copy-start = (f32[64,64]{1,0:T(8,128)S(1)}, f32[64,64]{1,0:T(8,128)}, u32[]{:S(2)}) copy-start(f32[64,64]{1,0:T(8,128)} %param.11) | copy-start | bytes 49156
  7.2 89.8 %copy-start.4 = (bf16[1,2048,128]{2,1,0:T(8,128)(2,1)S(1)}, bf16[1,2048,128]{2,1,0:T(8,128)(2,1)}, u32[]{:S(2)}) copy-start(bf16[1,2048,128]{2,1,0:T(8,128)(2,1)} %param.8) | copy-start | bytes 1572868
  7.2 190.6 %reduce-scatter.2.cloned.1.call-start = ((), (), s32[]{:S(2)}) async-start(), calls=%async_computation.1 | async-start | bytes 557056 | tf_op jit(solution)/shard_map/reduce_scatter | solution.py:75
  7.2 9.1 %collective-permute-start = (bf16[2048,128]{1,0:T(8,128)(2,1)}, bf16[2048,128]{1,0:T(8,128)(2,1)S(1)}, u32[]{:S(2)}, u32[]{:S(2)}) collective-permute-start(bf16[2048,128]{1,0:T(8,128)(2,1)} %bitcast.84), channel_id=1, source_target_pairs={{0,1},{1,2},{2,3},{3,4},{4,5},{5,6},{6,7},{7,8},{8,9},{9,10},{10,1... | collective-permute-start | bytes 1572872 | tf_op jit(solution)/shard_map/ppermute | solution.py:20
  16.4 9.2 %collective-permute-start.1 = (bf16[2048,128]{1,0:T(8,128)(2,1)S(1)}, bf16[2048,128]{1,0:T(8,128)(2,1)S(1)}, u32[]{:S(2)}, u32[]{:S(2)}) collective-permute-start(bf16[2048,128]{1,0:T(8,128)(2,1)S(1)} %collective-permute-done), channel_id=1, source_target_pairs={{0,1},{1,2},{2,3},{3,4},{4,5},{5,6},{6,7},{7,8},{8,9},{9,10},{10,1... | collective-permute-start | bytes 1572872 | tf_op jit(solution)/shard_map/ppermute | solution.py:20
  18.8 8.8 %collective-permute-start.8 = (bf16[2048,128]{1,0:T(8,128)(2,1)}, bf16[2048,128]{1,0:T(8,128)(2,1)S(1)}, u32[]{:S(2)}, u32[]{:S(2)}) collective-permute-start(bf16[2048,128]{1,0:T(8,128)(2,1)} %bitcast.85), channel_id=1, source_target_pairs={{1,0},{2,1},{3,2},{4,3},{5,4},{6,5},{7,6},{8,7},{9,8},{10,9},{11,1... | collective-permute-start | bytes 1572872 | tf_op jit(solution)/shard_map/ppermute | solution.py:22
  25.6 9.8 %collective-permute-start.2 = (bf16[2048,128]{1,0:T(8,128)(2,1)S(1)}, bf16[2048,128]{1,0:T(8,128)(2,1)S(1)}, u32[]{:S(2)}, u32[]{:S(2)}) collective-permute-start(bf16[2048,128]{1,0:T(8,128)(2,1)S(1)} %collective-permute-done.1), channel_id=1, source_target_pairs={{0,1},{1,2},{2,3},{3,4},{4,5},{5,6},{6,7},{7,8},{8,9},{9,10},{10,1... | collective-permute-start | bytes 1572872 | tf_op jit(solution)/shard_map/ppermute | solution.py:20
  27.6 8.6 %collective-permute-start.9 = (bf16[2048,128]{1,0:T(8,128)(2,1)S(1)}, bf16[2048,128]{1,0:T(8,128)(2,1)S(1)}, u32[]{:S(2)}, u32[]{:S(2)}) collective-permute-start(bf16[2048,128]{1,0:T(8,128)(2,1)S(1)} %collective-permute-done.8), channel_id=1, source_target_pairs={{1,0},{2,1},{3,2},{4,3},{5,4},{6,5},{7,6},{8,7},{9,8},{10,9},{11,1... | collective-permute-start | bytes 1572872 | tf_op jit(solution)/shard_map/ppermute | solution.py:22
  35.4 9.8 %collective-permute-start.3 = (bf16[2048,128]{1,0:T(8,128)(2,1)S(1)}, bf16[2048,128]{1,0:T(8,128)(2,1)S(1)}, u32[]{:S(2)}, u32[]{:S(2)}) collective-permute-start(bf16[2048,128]{1,0:T(8,128)(2,1)S(1)} %collective-permute-done.2), channel_id=1, source_target_pairs={{0,1},{1,2},{2,3},{3,4},{4,5},{5,6},{6,7},{7,8},{8,9},{9,10},{10,1... | collective-permute-start | bytes 1572872 | tf_op jit(solution)/shard_map/ppermute | solution.py:20
  36.2 9.2 %collective-permute-start.10 = (bf16[2048,128]{1,0:T(8,128)(2,1)S(1)}, bf16[2048,128]{1,0:T(8,128)(2,1)S(1)}, u32[]{:S(2)}, u32[]{:S(2)}) collective-permute-start(bf16[2048,128]{1,0:T(8,128)(2,1)S(1)} %collective-permute-done.9), channel_id=1, source_target_pairs={{1,0},{2,1},{3,2},{4,3},{5,4},{6,5},{7,6},{8,7},{9,8},{10,9},{11,1... | collective-permute-start | bytes 1572872 | tf_op jit(solution)/shard_map/ppermute | solution.py:22
  45.2 9.8 %collective-permute-start.4 = (bf16[2048,128]{1,0:T(8,128)(2,1)S(1)}, bf16[2048,128]{1,0:T(8,128)(2,1)S(1)}, u32[]{:S(2)}, u32[]{:S(2)}) collective-permute-start(bf16[2048,128]{1,0:T(8,128)(2,1)S(1)} %collective-permute-done.3), channel_id=1, source_target_pairs={{0,1},{1,2},{2,3},{3,4},{4,5},{5,6},{6,7},{7,8},{8,9},{9,10},{10,1... | collective-permute-start | bytes 1572872 | tf_op jit(solution)/shard_map/ppermute | solution.py:20
  46.2 9.9 %collective-permute-start.11 = (bf16[2048,128]{1,0:T(8,128)(2,1)S(1)}, bf16[2048,128]{1,0:T(8,128)(2,1)S(1)}, u32[]{:S(2)}, u32[]{:S(2)}) collective-permute-start(bf16[2048,128]{1,0:T(8,128)(2,1)S(1)} %collective-permute-done.10), channel_id=1, source_target_pairs={{1,0},{2,1},{3,2},{4,3},{5,4},{6,5},{7,6},{8,7},{9,8},{10,9},{11,1... | collective-permute-start | bytes 1572872 | tf_op jit(solution)/shard_map/ppermute | solution.py:22
  55.0 10.1 %collective-permute-start.5 = (bf16[2048,128]{1,0:T(8,128)(2,1)S(1)}, bf16[2048,128]{1,0:T(8,128)(2,1)S(1)}, u32[]{:S(2)}, u32[]{:S(2)}) collective-permute-start(bf16[2048,128]{1,0:T(8,128)(2,1)S(1)} %collective-permute-done.4), channel_id=1, source_target_pairs={{0,1},{1,2},{2,3},{3,4},{4,5},{5,6},{6,7},{7,8},{8,9},{9,10},{10,1... | collective-permute-start | bytes 1572872 | tf_op jit(solution)/shard_map/ppermute | solution.py:20
  56.8 9.9 %collective-permute-start.12 = (bf16[2048,128]{1,0:T(8,128)(2,1)S(1)}, bf16[2048,128]{1,0:T(8,128)(2,1)}, u32[]{:S(2)}, u32[]{:S(2)}) collective-permute-start(bf16[2048,128]{1,0:T(8,128)(2,1)S(1)} %collective-permute-done.11), channel_id=1, source_target_pairs={{1,0},{2,1},{3,2},{4,3},{5,4},{6,5},{7,6},{8,7},{9,8},{10,9},{11,1... | collective-permute-start | bytes 1572872 | tf_op jit(solution)/shard_map/ppermute | solution.py:22
  65.1 9.8 %collective-permute-start.6 = (bf16[2048,128]{1,0:T(8,128)(2,1)S(1)}, bf16[2048,128]{1,0:T(8,128)(2,1)}, u32[]{:S(2)}, u32[]{:S(2)}) collective-permute-start(bf16[2048,128]{1,0:T(8,128)(2,1)S(1)} %collective-permute-done.5), channel_id=1, source_target_pairs={{0,1},{1,2},{2,3},{3,4},{4,5},{5,6},{6,7},{7,8},{8,9},{9,10},{10,1... | collective-permute-start | bytes 1572872 | tf_op jit(solution)/shard_map/ppermute | solution.py:20
  66.7 10.0 %collective-permute-start.13 = (bf16[2048,128]{1,0:T(8,128)(2,1)}, bf16[2048,128]{1,0:T(8,128)(2,1)}, u32[]{:S(2)}, u32[]{:S(2)}) collective-permute-start(bf16[2048,128]{1,0:T(8,128)(2,1)} %collective-permute-done.12), channel_id=1, source_target_pairs={{1,0},{2,1},{3,2},{4,3},{5,4},{6,5},{7,6},{8,7},{9,8},{10,9},{11,1... | collective-permute-start | bytes 1572872 | tf_op jit(solution)/shard_map/ppermute | solution.py:22
  74.9 10.2 %collective-permute-start.7 = (bf16[2048,128]{1,0:T(8,128)(2,1)}, bf16[2048,128]{1,0:T(8,128)(2,1)}, u32[]{:S(2)}, u32[]{:S(2)}) collective-permute-start(bf16[2048,128]{1,0:T(8,128)(2,1)} %collective-permute-done.6), channel_id=1, source_target_pairs={{0,1},{1,2},{2,3},{3,4},{4,5},{5,6},{6,7},{7,8},{8,9},{9,10},{10,1... | collective-permute-start | bytes 1572872 | tf_op jit(solution)/shard_map/ppermute | solution.py:20
  76.8 28.2 %collective-permute-start.14 = (bf16[2048,128]{1,0:T(8,128)(2,1)}, bf16[2048,128]{1,0:T(8,128)(2,1)S(1)}, u32[]{:S(2)}, u32[]{:S(2)}) collective-permute-start(bf16[2048,128]{1,0:T(8,128)(2,1)} %collective-permute-done.13), channel_id=1, source_target_pairs={{1,0},{2,1},{3,2},{4,3},{5,4},{6,5},{7,6},{8,7},{9,8},{10,9},{11,1... | collective-permute-start | bytes 1572872 | tf_op jit(solution)/shard_map/ppermute | solution.py:22
  126.3 73.8 %copy-start.13 = (f32[1,2048]{1,0:T(1,128)S(1)}, f32[1,2048]{1,0:T(1,128)}, u32[]{:S(2)}) copy-start(f32[1,2048]{1,0:T(1,128)} %param.10) | copy-start | bytes 24580
  133.7 142.1 %all-gather.9.cloned.1.call-start = ((), (), s32[]{:S(2)}) async-start(), calls=%async_computation.3 | async-start | bytes 1081344 | tf_op jit(solution)/shard_map/all_gather | solution.py:31
  199.4 322.6 %all-gather.7.cloned.1.call-start = ((), (), s32[]{:S(2)}) async-start(), calls=%async_computation.2 | async-start | bytes 34603008 | tf_op jit(solution)/shard_map/all_gather | solution.py:31
  522.0 128.2 %copy-start.12 = (f32[128,64]{0,1:T(8,128)S(1)}, f32[128,64]{0,1:T(8,128)}, u32[]{:S(2)}) copy-start(f32[128,64]{0,1:T(8,128)} %convolution_negate_fusion) | copy-start | bytes 98308
  522.0 129.6 %copy-start.2 = (f32[2048,128]{1,0:T(8,128)S(1)}, f32[2048,128]{1,0:T(8,128)}, u32[]{:S(2)}) copy-start(f32[2048,128]{1,0:T(8,128)} %copy-done.1) | copy-start | bytes 3145732
  522.0 129.6 %copy-start.3 = (f32[2048,128]{1,0:T(8,128)S(1)}, f32[2048,128]{1,0:T(8,128)}, u32[]{:S(2)}) copy-start(f32[2048,128]{1,0:T(8,128)} %param.12) | copy-start | bytes 3145732
  (9 other events, 176.0 us)
Sparse Core Ops, SparseCore 0:
  133.8 63.9 reduce-scatter.1
  201.8 73.8 all-gather.8
  280.0 241.9 all-gather.6
